TPU v7x, 32 devices: a whole 2x2x4 slice. The times are simulated.
32 devices in a mesh: rep: 4 (over y, core), shard: 8 (over z, x).
Axes of the slice: x: 2, y: 2, z: 4, core: 2. Of those that a mesh axis runs over, the one named last changes fastest.
Arguments:
- weights: bfloat16 [4, 4096, 5120], P('rep', 'shard'), may hold values from -12 to 12
- warm_start: bfloat16 [4, 2, 16, 5120], P('rep'), may hold values from -4 to 4, as said below
Outputs:
- corrected: bfloat16 [4, 4096, 5120], P('rep', 'shard')
- factors: float32 [4, 2, 16, 5120], P('rep')
Inputs may be any that keep to these rules, and one draw needn't show every extreme that they name: `warm_start`: replicas whose indices differ only in bit 0 hold equal start vectors for matching 0, and replicas whose indices differ by 2 hold equal start vectors for matching 1.
All inputs are finite; a program needn't handle non-finite values.
Results may differ from a plain program's by a relative error of at most 0.0049.
Values sent between devices are 32-bit elements; how exact they have to be, the bound alone decides.
A program may use at most 64 MiB of HBM per device.

v0:
```python
import jax
import jax.numpy as jnp
from jax import lax
from jax.sharding import PartitionSpec as P

STEPS = 2


def partner(value, axis, stride):
    return lax.ppermute(value, axis, [(i, i ^ 1 << stride) for i in range(lax.axis_size(axis))])


def shards(weights, warm_start):
    current = weights[0]
    replica = lax.axis_index("rep")
    half_rep = lax.axis_size("rep") // 2
    top_bit = lax.axis_size("rep").bit_length() - 2
    factor_list = []
    for matching in range(STEPS):
        if matching == 0:
            bit_number = 0
            parity = 1.0 - 2.0 * (replica % 2).astype(jnp.float32)
        else:
            bit_number = top_bit
            parity = 1.0 - 2.0 * (replica // half_rep).astype(jnp.float32)
        starts = warm_start[0, matching]
        sketch = lax.dot_general(
            starts, current, (((1,), (1,)), ((), ())), preferred_element_type=jnp.float32
        )
        sketch_other = partner(sketch, "rep", bit_number)
        differ = parity * (sketch - sketch_other)
        gram_local = lax.dot_general(
            differ, differ, (((1,), (1,)), ((), ())), precision=lax.Precision.HIGHEST
        )
        gram_sum = lax.psum(gram_local, "shard")
        triangle = jnp.linalg.cholesky(gram_sum)
        basis_rows = lax.linalg.triangular_solve(triangle, differ, left_side=True, lower=True)
        signed = parity * jnp.dot(
            basis_rows.astype(jnp.bfloat16), current, preferred_element_type=jnp.float32
        )
        summed = lax.psum(signed, "shard")
        factors = summed + partner(summed, "rep", bit_number)
        change = lax.dot_general(
            basis_rows, factors, (((0,), (0,)), ((), ())), precision=lax.Precision.HIGHEST
        )
        current = (current.astype(jnp.float32) - 0.5 * parity * change).astype(jnp.bfloat16)
        factor_list.append(factors)
    return (current[None], jnp.stack(factor_list)[None])


def solution(mesh):
    placed = (P("rep", "shard", None), P("rep", None, None, None))
    return jax.shard_map(
        shards,
        mesh=mesh,
        in_specs=placed,
        out_specs=(P("rep", "shard", None), P("rep", None, None, None)),
        check_vma=False,
    )
```

profile of v0, /device:TPU:0, one launch (start us, length us, event | category | flops | bytes accessed | tf_op | source)
XLA Modules:
  0.0 259.3 jit_solution(16875092373942699540)
XLA Ops:
  7.2 0.0 all-reduce.3.cloned.1.call-start
  7.2 4.0 %fusion.2 = f32[16,512]{1,0:T(8,128)S(1)} fusion(bf16[1,512,5120]{2,1,0:T(8,128)(2,1)} %param.5, bf16[1,2,16,5120]{3,2,1,0:T(8,128)(2,1)} %param.6), kind=kOutput, calls=%fused_computation.6 | convolution fusion | flops 83886080 | bytes 5439488 | tf_op jit(solution)/shard_map/dot_general | solution.py:27
  11.2 0.5 collective-permute-start
  11.7 0.9 collective-permute-done
  12.6 0.1 fusion.13
  12.7 23.2 %psum.28 = f32[16,16]{0,1:T(8,128)S(1)} all-reduce(f32[16,16]{0,1:T(8,128)S(1)} %fusion.13), channel_id=1, replica_groups=mesh['rep'=4,'shard'=8] {'shard'}, use_global_device_ids=true, to_apply=%region_0.1 | all-reduce | flops 256 | bytes 2048 | tf_op jit(solution)/shard_map/psum | solution.py:35
  36.0 0.1 copy.5
  36.1 1.5 cholesky.44
  37.6 0.6 compare_reduce_fusion.1
  38.2 0.6 fusion.16
  38.9 1.2 custom-call.6
  40.1 0.2 fusion.12
  40.3 4.0 %convolution_multiply_fusion.1 = f32[16,5120]{1,0:T(8,128)} fusion(bf16[1,512,5120]{2,1,0:T(8,128)(2,1)} %param.5, f32[]{:T(128)S(6)} %sub.22, f32[16,512]{1,0:T(8,128)S(1)} %fusion.12), kind=kOutput, calls=%fused_computation.4 | convolution fusion | flops 83976192 | bytes 5603332 | tf_op jit(solution)/shard_map/dot_general | solution.py:38
  44.3 0.0 all-reduce.3.cloned.1.call-update
  44.4 0.0 all-reduce.5.cloned.1.call-start
  44.4 68.8 %all-reduce.3.cloned.1.call-done = f32[16,5120]{1,0:T(8,128)} async-done(((f32[16,5120]{1,0:T(8,128)}), f32[16,5120]{1,0:T(8,128)}) %all-reduce.3.cloned.1.call-update) | async-done | bytes 327696 | tf_op jit(solution)/shard_map/psum | solution.py:41
  113.2 0.0 collective-permute-start.1
  113.2 0.0 copy-start.2
  113.2 1.8 collective-permute-done.1
  115.0 10.8 %subtract_convert_fusion.1 = bf16[512,5120]{1,0:T(8,128)(2,1)S(1)} fusion(f32[16,512]{1,0:T(8,128)S(1)} %fusion.12, bf16[1,512,5120]{2,1,0:T(8,128)(2,1)} %param.5, f32[]{:T(128)S(6)} %mul.49, f32[16,5120]{1,0:T(8,128)} %all-reduce.3.cloned.1.call-done, f32[16,5120]{1,0:T(8,128)S(1)} %collective-permute-done.1), kind=kOutput, calls=%fused_computation.1 | convolution fusion | flops 513884160 | bytes 11173892 | tf_op jit(solution)/shard_map/dot_general | solution.py:43
  125.9 0.0 copy-start
  125.9 2.3 copy-done
  128.2 0.0 copy-done.2
  128.2 0.0 copy-start.1
  128.2 1.5 convolution_bitcast_fusion
  129.7 1.5 collective-permute-start.2
  131.2 2.4 collective-permute-done.2
  133.6 0.1 fusion.15
  133.8 19.9 %psum.30 = f32[16,16]{0,1:T(8,128)S(1)} all-reduce(f32[16,16]{0,1:T(8,128)S(1)} %fusion.15), channel_id=1, replica_groups=mesh['rep'=4,'shard'=8] {'shard'}, use_global_device_ids=true, to_apply=%region_4.7 | all-reduce | flops 256 | bytes 2048 | tf_op jit(solution)/shard_map/psum | solution.py:35
  153.7 0.1 copy.7
  153.7 1.5 cholesky.55
  155.2 0.6 compare_reduce_fusion
  155.9 0.6 fusion.17
  156.5 1.2 custom-call.7
  157.8 0.2 fusion.14
  158.0 4.0 %convolution_multiply_fusion = f32[16,5120]{1,0:T(8,128)} fusion(bf16[512,5120]{1,0:T(8,128)(2,1)} %copy-done, f32[]{:T(128)S(6)} %sub.26, f32[16,512]{1,0:T(8,128)S(1)} %fusion.14), kind=kOutput, calls=%fused_computation.3 | convolution fusion | flops 83976192 | bytes 5603332 | tf_op jit(solution)/shard_map/dot_general | solution.py:38
  162.0 0.0 all-reduce.5.cloned.1.call-update
  162.0 68.8 %all-reduce.5.cloned.1.call-done = f32[16,5120]{1,0:T(8,128)} async-done(((f32[16,5120]{1,0:T(8,128)}), f32[16,5120]{1,0:T(8,128)}) %all-reduce.5.cloned.1.call-update) | async-done | bytes 327696 | tf_op jit(solution)/shard_map/psum | solution.py:41
  230.8 1.5 collective-permute-start.3
  232.3 0.0 copy-done.1
  232.3 6.3 %collective-permute-done.3 = f32[16,5120]{1,0:T(8,128)S(1)} collective-permute-done((f32[16,5120]{1,0:T(8,128)}, f32[16,5120]{1,0:T(8,128)S(1)}, u32[]{:S(2)}, u32[]{:S(2)}) %collective-permute-start.3) | collective-permute-done | bytes 327712 | tf_op jit(solution)/shard_map/ppermute | solution.py:10
  238.6 1.0 add_bitcast_fusion
  239.6 0.9 maximum_bitcast_fusion
  240.5 11.9 %fusion = bf16[1,512,5120]{2,1,0:T(8,128)(2,1)} fusion(f32[16,512]{1,0:T(8,128)S(1)} %fusion.14, bf16[512,5120]{1,0:T(8,128)(2,1)} %copy-done, f32[]{:T(128)S(6)} %mul.57, f32[16,5120]{1,0:T(8,128)} %all-reduce.5.cloned.1.call-done, f32[16,5120]{1,0:T(8,128)S(1)} %collective-permute-done.3), kind=kOutput, calls=%fused_computation.2 | convolution fusion | flops 513884160 | bytes 11173892 | tf_op jit(solution)/shard_map/dot_general | solution.py:43
  (5 shorter events, 0.1 us)
Async XLA Ops:
  7.2 106.0 %all-reduce.3.cloned.1.call-start = ((), (), s32[]{:S(2)}) async-start(), calls=%async_computation | async-start | bytes 655360 | tf_op jit(solution)/shard_map/psum | solution.py:41
  11.2 1.4 collective-permute-start
  44.4 186.4 %all-reduce.5.cloned.1.call-start = ((), (), s32[]{:S(2)}) async-start(), calls=%async_computation.1 | async-start | bytes 655360 | tf_op jit(solution)/shard_map/psum | solution.py:41
  113.2 1.8 collective-permute-start.1
  113.2 15.0 %copy-start.2 = (bf16[1,2,16,5120]{3,2,1,0:T(8,128)(2,1)S(1)}, bf16[1,2,16,5120]{3,2,1,0:T(8,128)(2,1)}, u32[]{:S(2)}) copy-start(bf16[1,2,16,5120]{3,2,1,0:T(8,128)(2,1)} %param.6) | copy-start | bytes 983044
  125.9 2.4 copy-start
  128.2 104.0 %copy-start.1 = (f32[16,5120]{1,0:T(8,128)S(1)}, f32[16,5120]{1,0:T(8,128)}, u32[]{:S(2)}) copy-start(f32[16,5120]{1,0:T(8,128)} %all-reduce.3.cloned.1.call-done) | copy-start | bytes 983044
  129.7 3.9 %collective-permute-start.2 = (f32[16,512]{1,0:T(8,128)S(1)}, f32[16,512]{1,0:T(8,128)S(1)}, u32[]{:S(2)}, u32[]{:S(2)}) collective-permute-start(f32[16,512]{1,0:T(8,128)S(1)} %convolution_bitcast_fusion), channel_id=1, source_target_pairs={{0,16},{8,24},{16,0},{24,8},{1,17},{9,25},{17,1},{25,9},{2,18},{10... | collective-permute-start | bytes 98312 | tf_op jit(solution)/shard_map/ppermute | solution.py:10
  230.8 7.8 %collective-permute-start.3 = (f32[16,5120]{1,0:T(8,128)}, f32[16,5120]{1,0:T(8,128)S(1)}, u32[]{:S(2)}, u32[]{:S(2)}) collective-permute-start(f32[16,5120]{1,0:T(8,128)} %all-reduce.5.cloned.1.call-done), channel_id=1, source_target_pairs={{0,16},{8,24},{16,0},{24,8},{1,17},{9,25},{17,1},{25,9},{2,18},{10... | collective-permute-start | bytes 983048 | tf_op jit(solution)/shard_map/ppermute | solution.py:10
Sparse Core Ops, SparseCore 0:
  44.5 68.6 all-reduce.2
  162.2 68.5 all-reduce.4
where the time goes:
time: 260 us; the launch traced here: 259 us
  waiting for transfers between devices  149 us (57%)
  blocking collectives  43.1 us (17%)
  matrix products  37 us (14%)
  between operations  14.1 us (5%)
  other arithmetic  9.97 us (4%)
  starting transfers between devices  3.53 us (1%)
    psum x2, waiting for transfers between devices, shards(): summed = lax.psum(signed, 'shard')  138 us
    psum x2, blocking collectives, shards(): gram_sum = lax.psum(gram_local, 'shard')  43.1 us
    dot_general x2, matrix products, shards(): lax.dot_general(basis_rows, factors, (((0,), (0,)), ((), ())), precision=...  22.7 us
    ppermute x4, waiting for transfers between devices, partner(): lax.ppermute(value, axis, [(i, i ^ 1 << stride) for i in range(lax.axis_s...  11.5 us
    dot_general x2, matrix products, shards(): jnp.dot(basis_rows.astype(jnp.bfloat16), current, preferred_element_type=...  8.02 us
    dot_general x2, matrix products, shards(): lax.dot_general(starts, current, (((1,), (1,)), ((), ())), preferred_elem...  5.49 us
  transfers between devices with their start and end apart: 6, of which 6 were waited for; matrix products, arithmetic and copies ran while one was open for 0% of the time, Pallas kernels for 0%

commit v1 on v0

--- a/solution.py
+++ b/solution.py
@@ -32,7 +32,7 @@
         gram_local = lax.dot_general(
             differ, differ, (((1,), (1,)), ((), ())), precision=lax.Precision.HIGHEST
         )
-        gram_sum = lax.psum(gram_local, "shard")
+        gram_sum = jnp.sum(lax.all_gather(gram_local, "shard"), axis=0)
         triangle = jnp.linalg.cholesky(gram_sum)
         basis_rows = lax.linalg.triangular_solve(triangle, differ, left_side=True, lower=True)
         signed = parity * jnp.dot(

time: 260 us -> 285 us (1.096)
  blocking collectives: 43.1 us -> 62.8 us
  waiting for transfers between devices: 149 us -> 155 us
    all_gather x0 -> x2, blocking collectives: none -> 62.8 us  [shards(): gram_sum = jnp.sum(lax.all_gather(gram_local, 'shard'), axis=0)]
    psum x2 -> x0, blocking collectives: 43.1 us -> none  [shards(): gram_sum = lax.psum(gram_local, 'shard')]
    psum x2, waiting for transfers between devices: 138 us -> 143 us  [shards(): summed = lax.psum(signed, 'shard')]
where the time goes in v1:
time: 285 us; the launch traced here: 284 us
  waiting for transfers between devices  155 us (54%)
  blocking collectives  62.8 us (22%)
  matrix products  37 us (13%)
  between operations  14.1 us (5%)
  other arithmetic  10 us (4%)
  starting transfers between devices  3.54 us (1%)
    psum x2, waiting for transfers between devices, shards(): summed = lax.psum(signed, 'shard')  143 us
    all_gather x2, blocking collectives, shards(): gram_sum = jnp.sum(lax.all_gather(gram_local, 'shard'), axis=0)  62.8 us
    dot_general x2, matrix products, shards(): lax.dot_general(basis_rows, factors, (((0,), (0,)), ((), ())), precision=...  22.7 us
    ppermute x4, waiting for transfers between devices, partner(): lax.ppermute(value, axis, [(i, i ^ 1 << stride) for i in range(lax.axis_s...  11.5 us
    dot_general x2, matrix products, shards(): jnp.dot(basis_rows.astype(jnp.bfloat16), current, preferred_element_type=...  8.02 us
  transfers between devices with their start and end apart: 6, of which 6 were waited for; matrix products, arithmetic and copies ran while one was open for 0% of the time, Pallas kernels for 0%

profile of v1, /device:TPU:0, one launch (start us, length us, event | category | flops | bytes accessed | tf_op | source)
XLA Modules:
  0.0 284.4 jit_solution(141980312301753384)
XLA Ops:
  7.2 0.0 all-reduce.3.cloned.1.call-start
  7.2 4.0 %fusion.2 = f32[16,512]{1,0:T(8,128)S(1)} fusion(bf16[1,512,5120]{2,1,0:T(8,128)(2,1)} %param.5, bf16[1,2,16,5120]{3,2,1,0:T(8,128)(2,1)} %param.6), kind=kOutput, calls=%fused_computation.6 | convolution fusion | flops 83886080 | bytes 5439488 | tf_op jit(solution)/shard_map/dot_general | solution.py:27
  11.2 0.5 collective-permute-start
  11.7 0.9 collective-permute-done
  12.6 0.1 fusion.13
  12.7 32.2 %all-gather = f32[128,16]{1,0:T(8,128)S(1)} all-gather(f32[16,16]{1,0:T(8,128)S(1)} %fusion.13), channel_id=2, replica_groups=mesh['rep'=4,'shard'=8] {'shard'}, dimensions={0}, use_global_device_ids=true | all-gather | bytes 9216 | tf_op jit(solution)/shard_map/all_gather | solution.py:35
  45.0 0.1 copy.6
  45.1 1.4 cholesky.44
  46.6 0.6 compare_reduce_fusion.1
  47.2 0.6 fusion.16
  47.9 1.2 custom-call.6
  49.1 0.2 fusion.12
  49.3 4.0 %convolution_multiply_fusion.1 = f32[16,5120]{1,0:T(8,128)} fusion(bf16[1,512,5120]{2,1,0:T(8,128)(2,1)} %param.5, f32[]{:T(128)S(6)} %sub.22, f32[16,512]{1,0:T(8,128)S(1)} %fusion.12), kind=kOutput, calls=%fused_computation.4 | convolution fusion | flops 83976192 | bytes 5603332 | tf_op jit(solution)/shard_map/dot_general | solution.py:38
  53.3 0.0 all-reduce.3.cloned.1.call-update
  53.4 0.0 all-reduce.5.cloned.1.call-start
  53.4 72.4 %all-reduce.3.cloned.1.call-done = f32[16,5120]{1,0:T(8,128)} async-done(((f32[16,5120]{1,0:T(8,128)}), f32[16,5120]{1,0:T(8,128)}) %all-reduce.3.cloned.1.call-update) | async-done | bytes 327696 | tf_op jit(solution)/shard_map/psum | solution.py:41
  125.8 0.0 collective-permute-start.1
  125.8 0.0 copy-start.2
  125.8 1.8 collective-permute-done.1
  127.6 10.8 %subtract_convert_fusion.1 = bf16[512,5120]{1,0:T(8,128)(2,1)S(1)} fusion(f32[16,512]{1,0:T(8,128)S(1)} %fusion.12, bf16[1,512,5120]{2,1,0:T(8,128)(2,1)} %param.5, f32[]{:T(128)S(6)} %mul.49, f32[16,5120]{1,0:T(8,128)} %all-reduce.3.cloned.1.call-done, f32[16,5120]{1,0:T(8,128)S(1)} %collective-permute-done.1), kind=kOutput, calls=%fused_computation.1 | convolution fusion | flops 513884160 | bytes 11173892 | tf_op jit(solution)/shard_map/dot_general | solution.py:43
  138.5 0.0 copy-start
  138.5 2.3 copy-done
  140.8 0.0 copy-done.2
  140.8 0.0 copy-start.1
  140.8 1.5 convolution_bitcast_fusion
  142.3 1.5 collective-permute-start.2
  143.8 2.4 collective-permute-done.2
  146.2 0.1 fusion.15
  146.3 30.6 %all-gather.1 = f32[128,16]{1,0:T(8,128)S(1)} all-gather(f32[16,16]{1,0:T(8,128)S(1)} %fusion.15), channel_id=3, replica_groups=mesh['rep'=4,'shard'=8] {'shard'}, dimensions={0}, use_global_device_ids=true | all-gather | bytes 9216 | tf_op jit(solution)/shard_map/all_gather | solution.py:35
  176.9 0.1 copy.7
  177.0 1.5 cholesky.55
  178.5 0.6 compare_reduce_fusion
  179.1 0.6 fusion.17
  179.8 1.2 custom-call.7
  181.0 0.2 fusion.14
  181.3 4.0 %convolution_multiply_fusion = f32[16,5120]{1,0:T(8,128)} fusion(bf16[512,5120]{1,0:T(8,128)(2,1)} %copy-done, f32[]{:T(128)S(6)} %sub.26, f32[16,512]{1,0:T(8,128)S(1)} %fusion.14), kind=kOutput, calls=%fused_computation.3 | convolution fusion | flops 83976192 | bytes 5603332 | tf_op jit(solution)/shard_map/dot_general | solution.py:38
  185.3 0.0 all-reduce.5.cloned.1.call-update
  185.3 70.7 %all-reduce.5.cloned.1.call-done = f32[16,5120]{1,0:T(8,128)} async-done(((f32[16,5120]{1,0:T(8,128)}), f32[16,5120]{1,0:T(8,128)}) %all-reduce.5.cloned.1.call-update) | async-done | bytes 327696 | tf_op jit(solution)/shard_map/psum | solution.py:41
  256.0 1.5 collective-permute-start.3
  257.4 0.0 copy-done.1
  257.5 6.3 %collective-permute-done.3 = f32[16,5120]{1,0:T(8,128)S(1)} collective-permute-done((f32[16,5120]{1,0:T(8,128)}, f32[16,5120]{1,0:T(8,128)S(1)}, u32[]{:S(2)}, u32[]{:S(2)}) %collective-permute-start.3) | collective-permute-done | bytes 327712 | tf_op jit(solution)/shard_map/ppermute | solution.py:10
  263.8 1.0 add_bitcast_fusion
  264.8 0.9 maximum_bitcast_fusion
  265.7 11.9 %fusion = bf16[1,512,5120]{2,1,0:T(8,128)(2,1)} fusion(f32[16,512]{1,0:T(8,128)S(1)} %fusion.14, bf16[512,5120]{1,0:T(8,128)(2,1)} %copy-done, f32[]{:T(128)S(6)} %mul.57, f32[16,5120]{1,0:T(8,128)} %all-reduce.5.cloned.1.call-done, f32[16,5120]{1,0:T(8,128)S(1)} %collective-permute-done.3), kind=kOutput, calls=%fused_computation.2 | convolution fusion | flops 513884160 | bytes 11173892 | tf_op jit(solution)/shard_map/dot_general | solution.py:43
  (7 shorter events, 0.1 us)
Async XLA Ops:
  7.2 118.6 %all-reduce.3.cloned.1.call-start = ((), (), s32[]{:S(2)}) async-start(), calls=%async_computation | async-start | bytes 655360 | tf_op jit(solution)/shard_map/psum | solution.py:41
  11.2 1.4 collective-permute-start
  53.4 202.6 %all-reduce.5.cloned.1.call-start = ((), (), s32[]{:S(2)}) async-start(), calls=%async_computation.1 | async-start | bytes 655360 | tf_op jit(solution)/shard_map/psum | solution.py:41
  125.8 1.8 collective-permute-start.1
  125.8 15.0 %copy-start.2 = (bf16[1,2,16,5120]{3,2,1,0:T(8,128)(2,1)S(1)}, bf16[1,2,16,5120]{3,2,1,0:T(8,128)(2,1)}, u32[]{:S(2)}) copy-start(bf16[1,2,16,5120]{3,2,1,0:T(8,128)(2,1)} %param.6) | copy-start | bytes 983044
  138.5 2.4 copy-start
  140.8 116.6 %copy-start.1 = (f32[16,5120]{1,0:T(8,128)S(1)}, f32[16,5120]{1,0:T(8,128)}, u32[]{:S(2)}) copy-start(f32[16,5120]{1,0:T(8,128)} %all-reduce.3.cloned.1.call-done) | copy-start | bytes 983044
  142.3 3.9 %collective-permute-start.2 = (f32[16,512]{1,0:T(8,128)S(1)}, f32[16,512]{1,0:T(8,128)S(1)}, u32[]{:S(2)}, u32[]{:S(2)}) collective-permute-start(f32[16,512]{1,0:T(8,128)S(1)} %convolution_bitcast_fusion), channel_id=1, source_target_pairs={{0,16},{8,24},{16,0},{24,8},{1,17},{9,25},{17,1},{25,9},{2,18},{10... | collective-permute-start | bytes 98312 | tf_op jit(solution)/shard_map/ppermute | solution.py:10
  256.0 7.8 %collective-permute-start.3 = (f32[16,5120]{1,0:T(8,128)}, f32[16,5120]{1,0:T(8,128)S(1)}, u32[]{:S(2)}, u32[]{:S(2)}) collective-permute-start(f32[16,5120]{1,0:T(8,128)} %all-reduce.5.cloned.1.call-done), channel_id=1, source_target_pairs={{0,16},{8,24},{16,0},{24,8},{1,17},{9,25},{17,1},{25,9},{2,18},{10... | collective-permute-start | bytes 983048 | tf_op jit(solution)/shard_map/ppermute | solution.py:10
Sparse Core Ops, SparseCore 0:
  53.5 72.2 all-reduce.2
  185.4 70.5 all-reduce.4
